TPU v7x, 512 devices: a whole 4x8x8 slice. The times are simulated.
512 devices in a mesh: row: 16 (over z, core), col: 32 (over y, x).
Axes of the slice: x: 4, y: 8, z: 8, core: 2. Of those that a mesh axis runs over, the one named last changes fastest.
Arguments:
- config: float32 [6, 65536], P(None, ('row', 'col')), as said below
- start: float32 [6, 65536], P(None, ('row', 'col')), may hold values from -6 to 6
- tile_list: int32 [16, 32, 8, 5], P('row', 'col'), may hold values from -1 to 31, as said below
- tile_count: int32 [16, 32], P('row', 'col'), may hold values from 1 to 8, as said below
Outputs:
- coefficients: float32 [4], replicated
- mode: float32 [6, 65536], P(None, ('row', 'col'))
Inputs may be any that keep to these rules, and one draw needn't show every extreme that they name: `tile_list`: entry k of device (r, c) is used when k < tile_count[r, c]; its first value is a row tile 0 to 31, its second a column tile 0 to 15, the last three are offsets in -1, 0, 1, not all zero. Unused entries hold values of the same law. `tile_count`: some device uses all 8 entries. `config`: rows 3 to 5 are unit vectors. No two ellipsoids intersect, within a tile or across tiles placed by a list entry's offsets.
All inputs are finite; a program needn't handle non-finite values.
Results may differ from a plain program's by a relative error of at most 0.0003.
Values sent between devices are 32-bit elements; how exact they have to be, the bound alone decides.
A program may use at most 64 MiB of HBM per device.

v0:
```python
import math

import jax
import jax.numpy as jnp
from jax import lax
from jax.sharding import PartitionSpec as P

chi_shape = 0.8
chi_energy = (math.sqrt(5.0) - 1.0) / (math.sqrt(5.0) + 1.0)
well_depth = 0.005
cutoff_sq = 20.25
norm_eps = 1e-06


def rotate(heading, turn):
    moved = heading + jnp.cross(turn, heading, axis=0)
    return moved / jnp.sqrt(jnp.sum(moved * moved, axis=0, keepdims=True))


def place(frame, dof):
    return (frame[:3] + dof[:3], rotate(frame[3:], dof[3:]))


def pair_energy(separation, left_axis, right_axis):
    distance_sq = jnp.sum(separation * separation, axis=0)
    distance = jnp.sqrt(distance_sq)
    direction = separation / distance
    along_left = jnp.sum(direction * left_axis, axis=0)
    along_right = jnp.sum(direction * right_axis, axis=0)
    cosine = jnp.sum(left_axis * right_axis, axis=0)
    summed_sq = (along_left + along_right) ** 2
    differ_sq = (along_left - along_right) ** 2
    shape_term = 1.0 - 0.5 * chi_shape * (
        summed_sq / (1.0 + chi_shape * cosine) + differ_sq / (1.0 - chi_shape * cosine)
    )
    contact = 1.0 / jnp.sqrt(shape_term)
    strength_one = 1.0 / jnp.sqrt(1.0 - chi_shape * chi_shape * cosine * cosine)
    strength_two = 1.0 - 0.5 * chi_energy * (
        summed_sq / (1.0 + chi_energy * cosine) + differ_sq / (1.0 - chi_energy * cosine)
    )
    reduced = 1.0 / (distance - contact + 1.0)
    sixth = reduced**6
    switch = jnp.maximum(1.0 - distance_sq / cutoff_sq, 0.0) ** 3
    return (
        4.0
        * well_depth
        * strength_one
        * strength_two
        * strength_two
        * (sixth * sixth - sixth)
        * switch
    )


def cross_energy(dof_left, dof_right, left_frame, right_frame, brick_shift):
    left_centre, left_axis = place(left_frame, dof_left)
    right_centre, right_axis = place(right_frame, dof_right)
    separation = right_centre[:, None, :] + brick_shift[:, None, None] - left_centre[:, :, None]
    return jnp.sum(pair_energy(separation, left_axis[:, :, None], right_axis[:, None, :]))


def own_energy(dof, frame):
    centre, heading = place(frame, dof)
    ordinal = lax.iota(jnp.int32, frame.shape[1])
    upper_mask = (ordinal[:, None] < ordinal[None, :]).astype(frame.dtype)
    diagonal = (ordinal[:, None] == ordinal[None, :]).astype(frame.dtype)
    separation = centre[:, None, :] - centre[:, :, None]
    lifted = separation + jnp.stack([0.0 * diagonal, 0.0 * diagonal, 8.0 * diagonal])
    return jnp.sum(upper_mask * pair_energy(lifted, heading[:, :, None], heading[:, None, :]))


def cross_product(left_frame, right_frame, left_tangent, right_tangent, brick_shift):

    def cross_gradient(dof_left, dof_right):
        return jax.grad(cross_energy, argnums=(0, 1))(
            dof_left, dof_right, left_frame, right_frame, brick_shift
        )

    anchor = (jnp.zeros_like(left_tangent), jnp.zeros_like(right_tangent))
    _, tangent = jax.jvp(cross_gradient, anchor, (left_tangent, right_tangent))
    return tangent


def own_product(frame, vector):

    def own_gradient(dof):
        return jax.grad(own_energy)(dof, frame)

    _, tangent = jax.jvp(own_gradient, (jnp.zeros_like(vector),), (vector,))
    return tangent


def local(config, start, tile_list, tile_count):
    member = config.shape[1]
    row_devices = lax.axis_size("row")
    col_devices = lax.axis_size("col")
    total_entries = 6 * member * row_devices * col_devices
    period = jnp.array([5.0, 5.0, 3.5 * (member // 16)], dtype=jnp.float32)
    row_frames = lax.all_gather(config, "col", axis=1, tiled=True)
    col_frames = lax.all_gather(config, "row", axis=1, tiled=True)
    entries = tile_list[0, 0]
    used = tile_count[0, 0]
    row_rank = lax.axis_index("row")
    col_rank = lax.axis_index("col")

    def apply_hessian(vector):
        own_term = own_product(config, vector)
        row_vectors = lax.all_gather(vector, "col", axis=1, tiled=True)
        col_vectors = lax.all_gather(vector, "row", axis=1, tiled=True)

        def visit(slot, totals):
            row_total, col_total = totals
            entry = entries[slot]
            left = entry[0] * member
            right = entry[1] * member
            brick_shift = entry[2:5].astype(jnp.float32) * period
            left_out, right_out = cross_product(
                lax.dynamic_slice_in_dim(row_frames, left, member, 1),
                lax.dynamic_slice_in_dim(col_frames, right, member, 1),
                lax.dynamic_slice_in_dim(row_vectors, left, member, 1),
                lax.dynamic_slice_in_dim(col_vectors, right, member, 1),
                brick_shift,
            )
            row_total = lax.dynamic_update_slice_in_dim(
                row_total, lax.dynamic_slice_in_dim(row_total, left, member, 1) + left_out, left, 1
            )
            col_total = lax.dynamic_update_slice_in_dim(
                col_total,
                lax.dynamic_slice_in_dim(col_total, right, member, 1) + right_out,
                right,
                1,
            )
            return (row_total, col_total)

        row_total, col_total = lax.fori_loop(
            0, used, visit, (jnp.zeros_like(row_vectors), jnp.zeros_like(col_vectors))
        )
        layout = jnp.zeros((6, row_devices, col_devices, member), jnp.float32)
        layout = lax.dynamic_update_slice(
            layout, row_total.reshape(6, 1, col_devices, member), (0, row_rank, 0, 0)
        )
        column = lax.dynamic_slice(layout, (0, 0, col_rank, 0), (6, row_devices, 1, member))
        layout = lax.dynamic_update_slice(
            layout, column + col_total.reshape(6, row_devices, 1, member), (0, 0, col_rank, 0)
        )
        summed = lax.psum(layout.reshape(6, row_devices * col_devices * member), ("row", "col"))
        mine = lax.dynamic_slice_in_dim(
            summed, (row_rank * col_devices + col_rank) * member, member, 1
        )
        outcome = own_term + mine
        return outcome

    def mean_one(values):
        return lax.psum(jnp.sum(values), ("row", "col")) / total_entries

    def next_vector(image, basis):
        alpha = mean_one(basis * image)
        residual = image - alpha * basis
        residual_sq = mean_one(residual * residual)
        beta = jnp.sqrt(residual_sq + norm_eps)
        return (alpha, beta, residual / beta)

    first = start / jnp.sqrt(mean_one(start * start) + norm_eps)
    alpha_one, beta_one, second = next_vector(apply_hessian(first), first)
    alpha_two, beta_two, mode = next_vector(apply_hessian(second) - beta_one * first, second)
    return (jnp.stack([alpha_one, beta_one, alpha_two, beta_two]), mode)


def solution(mesh):
    placed = (
        P(None, ("row", "col")),
        P(None, ("row", "col")),
        P("row", "col", None, None),
        P("row", "col"),
    )
    return jax.shard_map(
        local, mesh=mesh, in_specs=placed, out_specs=(P(), P(None, ("row", "col"))), check_vma=False
    )
```

profile of v0, /device:TPU:1, one launch (start us, length us, event | category | flops | bytes accessed | tf_op | source)
XLA Modules:
  0.0 1337.7 jit_solution(3834644686289660931)
XLA Ops:
  7.2 32.5 %all_gather.18 = f32[6,4096]{1,0:T(8,128)S(1)} all-gather(f32[6,128]{1,0:T(8,128)} %param.24), channel_id=1, replica_groups=mesh['row'=16,'col'=32] {'col'}, dimensions={1}, use_global_device_ids=true | all-gather | bytes 101376 | tf_op jit(solution)/shard_map/all_gather | solution.py:99
  39.8 32.3 %all_gather.20 = f32[6,2048]{1,0:T(8,128)S(1)} all-gather(f32[6,128]{1,0:T(8,128)} %param.24), channel_id=1, replica_groups=mesh['row'=16,'col'=32] {'row'}, dimensions={1}, use_global_device_ids=true | all-gather | bytes 52224 | tf_op jit(solution)/shard_map/all_gather | solution.py:100
  72.0 1.3 multiply_reduce_fusion.39
  73.3 94.3 %psum.49 = f32[]{:T(128)} all-reduce(f32[]{:T(128)} %multiply_reduce_fusion.39), channel_id=1, replica_groups=mesh['row'=16,'col'=32] {'row','col'}, use_global_device_ids=true, to_apply=%region_1.0 | all-reduce | flops 1 | bytes 8 | tf_op jit(solution)/shard_map/psum | solution.py:154
  168.3 0.7 broadcast_divide_fusion.23
  169.0 29.6 %all_gather.19 = f32[6,4096]{1,0:T(8,128)S(1)} all-gather(f32[6,128]{1,0:T(8,128)S(1)} %broadcast_divide_fusion.23), channel_id=1, replica_groups=mesh['row'=16,'col'=32] {'col'}, dimensions={1}, use_global_device_ids=true | all-gather | bytes 101376 | tf_op jit(solution)/shard_map/all_gather | solution.py:108
  198.6 24.4 %all_gather.21 = f32[6,2048]{1,0:T(8,128)S(1)} all-gather(f32[6,128]{1,0:T(8,128)S(1)} %broadcast_divide_fusion.23), channel_id=1, replica_groups=mesh['row'=16,'col'=32] {'row'}, dimensions={1}, use_global_device_ids=true | all-gather | bytes 52224 | tf_op jit(solution)/shard_map/all_gather | solution.py:109
  223.0 0.8 copy.12
  223.7 7.7 while.26
  226.6 0.7 multiply_bitcast_fusion.4
  227.9 0.7 fusion.376
  229.2 0.6 add_reduce_fusion.39
  231.8 2.6 dynamic_update_slice.25
  234.3 2.2 copy.30
  240.6 317.0 %all-reduce.24.cloned.1.call-done = f32[6,65536]{1,0:T(8,128)} async-done(((f32[6,65536]{1,0:T(8,128)}), f32[6,65536]{1,0:T(8,128)}) %all-reduce.24.cloned.1.call-update) | async-done | bytes 1572880 | tf_op jit(solution)/shard_map/psum | solution.py:146
  557.6 1.3 multiply_reduce_fusion.38
  558.9 96.5 %psum.51 = f32[]{:T(128)} all-reduce(f32[]{:T(128)} %get-tuple-element.458), channel_id=1, replica_groups=mesh['row'=16,'col'=32] {'row','col'}, use_global_device_ids=true, to_apply=%region_58.63 | all-reduce | flops 1 | bytes 8 | tf_op jit(solution)/shard_map/psum | solution.py:154
  656.0 0.6 multiply_reduce_fusion.37
  656.6 95.0 %psum.52 = f32[]{:T(128)} all-reduce(f32[]{:T(128)} %multiply_reduce_fusion.37), channel_id=1, replica_groups=mesh['row'=16,'col'=32] {'row','col'}, use_global_device_ids=true, to_apply=%region_60.65 | all-reduce | flops 1 | bytes 8 | tf_op jit(solution)/shard_map/psum | solution.py:154
  752.3 29.4 %all_gather.22 = f32[6,4096]{1,0:T(8,128)S(1)} all-gather(f32[6,128]{1,0:T(8,128)S(1)} %broadcast_divide_fusion.22), channel_id=1, replica_groups=mesh['row'=16,'col'=32] {'col'}, dimensions={1}, use_global_device_ids=true | all-gather | bytes 101376 | tf_op jit(solution)/shard_map/all_gather | solution.py:108
  781.8 24.5 %all_gather.23 = f32[6,2048]{1,0:T(8,128)S(1)} all-gather(f32[6,128]{1,0:T(8,128)S(1)} %broadcast_divide_fusion.22), channel_id=1, replica_groups=mesh['row'=16,'col'=32] {'row'}, dimensions={1}, use_global_device_ids=true | all-gather | bytes 52224 | tf_op jit(solution)/shard_map/all_gather | solution.py:109
  806.3 7.0 while.27
  809.8 0.7 fusion.387
  811.0 0.6 add_reduce_fusion.41
  813.6 2.6 dynamic_update_slice.27
  816.2 2.2 copy.29
  821.4 313.8 %all-reduce.26.cloned.1.call-done = f32[6,65536]{1,0:T(8,128)} async-done(((f32[6,65536]{1,0:T(8,128)}), f32[6,65536]{1,0:T(8,128)}) %all-reduce.26.cloned.1.call-update) | async-done | bytes 1572880 | tf_op jit(solution)/shard_map/psum | solution.py:146
  1135.1 1.3 multiply_reduce_fusion.36
  1136.4 96.5 %psum.54 = f32[]{:T(128)} all-reduce(f32[]{:T(128)} %get-tuple-element.446), channel_id=1, replica_groups=mesh['row'=16,'col'=32] {'row','col'}, use_global_device_ids=true, to_apply=%region_116.0 | all-reduce | flops 1 | bytes 8 | tf_op jit(solution)/shard_map/psum | solution.py:154
  1233.6 0.6 multiply_reduce_fusion.35
  1234.2 94.8 %psum.55 = f32[]{:T(128)} all-reduce(f32[]{:T(128)} %multiply_reduce_fusion.35), channel_id=1, replica_groups=mesh['row'=16,'col'=32] {'row','col'}, use_global_device_ids=true, to_apply=%region_118.0 | all-reduce | flops 1 | bytes 8 | tf_op jit(solution)/shard_map/psum | solution.py:154
  1329.7 0.6 broadcast_divide_fusion.21
  (146 shorter events, 13.6 us)
Async XLA Ops:
  7.2 550.4 %all-reduce.24.cloned.1.call-start = ((), (), s32[]{:S(2)}) async-start(), calls=%async_computation | async-start | bytes 4194304 | tf_op jit(solution)/shard_map/psum | solution.py:146
  236.6 0.7 copy-start.1
  236.6 898.5 %all-reduce.26.cloned.1.call-start = ((), (), s32[]{:S(2)}) async-start(), calls=%async_computation.1 | async-start | bytes 4194304 | tf_op jit(solution)/shard_map/psum | solution.py:146
  239.1 318.6 %copy-start = (f32[6,128]{1,0:T(8,128)S(1)}, f32[6,128]{1,0:T(8,128)}, u32[]{:S(2)}) copy-start(f32[6,128]{1,0:T(8,128)} %param.25) | copy-start | bytes 9220
  239.5 566.7 %copy-start.2 = (f32[1,3]{1,0:T(1,128)S(1)}, f32[1,3]{1,0:T(1,128)}, u32[]{:S(2)}) copy-start(f32[1,3]{1,0:T(1,128)} %get-tuple-element.1266) | copy-start | bytes 40
Sparse Core Ops, SparseCore 0:
  236.7 320.8 all-reduce.23
  818.6 316.5 all-reduce.25
where the time goes:
time: 1340 us
  blocking collectives  650 us (49%)
  waiting for transfers between devices  631 us (47%)
  other arithmetic  20.8 us (2%)
  between operations  17.7 us (1%)
    psum x2, waiting for transfers between devices, apply_hessian(): lax.psum(layout.reshape(6, row_devices * col_devices * member), ('row', '...  631 us
    psum x5, blocking collectives, mean_one(): return lax.psum(jnp.sum(values), ('row', 'col')) / total_entries  477 us
    all_gather x2, blocking collectives, apply_hessian(): row_vectors = lax.all_gather(vector, 'col', axis=1, tiled=True)  59 us
    all_gather x2, blocking collectives, apply_hessian(): col_vectors = lax.all_gather(vector, 'row', axis=1, tiled=True)  48.9 us
    all_gather x1, blocking collectives, local(): row_frames = lax.all_gather(config, 'col', axis=1, tiled=True)  32.5 us
    all_gather x1, blocking collectives, local(): col_frames = lax.all_gather(config, 'row', axis=1, tiled=True)  32.3 us
  transfers between devices with their start and end apart: 2, of which 2 were waited for; matrix products, arithmetic and copies ran while one was open for 0% of the time, Pallas kernels for 0%

commit v1 on v0

v1 whole, which is shorter than its diff:
```python
import functools
import math

import jax
import jax.numpy as jnp
from jax import lax
from jax.experimental import pallas as pl
from jax.experimental.pallas import tpu as pltpu
from jax.sharding import PartitionSpec as P

MESH = pl.DeviceIdType.MESH
chi_shape = 0.8
chi_energy = (math.sqrt(5.0) - 1.0) / (math.sqrt(5.0) + 1.0)
well_depth = 0.005
cutoff_sq = 20.25
norm_eps = 1e-06
LANES = 128
CHUNK = 8
KEPT = 20


def dot3(a, b):
    return a[0] * b[0] + a[1] * b[1] + a[2] * b[2]


def cross3(a, b):
    return (
        a[1] * b[2] - a[2] * b[1],
        a[2] * b[0] - a[0] * b[2],
        a[0] * b[1] - a[1] * b[0],
    )


def anisotropy(x, spread, tau, A, B, c, norm, twice_cab, prod_tau):
    t = (2.0 * x) * spread * tau
    h = 0.5 * t * (norm - x * twice_cab)
    xc = x * c
    gA = t * (xc * B - A)
    gB = t * (xc * A - B)
    e = (2.0 * x * x) * spread
    gc = e * (prod_tau - c * h)
    gAB = xc * t
    gAc = e * (c * gA + B * tau)
    gBc = e * (c * gB + A * tau)
    gcc = e * (2.0 * c * gc - h)
    tau2 = 2.0 * tau
    gx = tau2 * h
    first = (gx, gA, gB, gc)
    second = {
        (0, 0): -2.0 * tau2 * gx,
        (0, 1): -tau2 * gA,
        (0, 2): -tau2 * gB,
        (0, 3): -tau2 * gc,
        (1, 1): -t,
        (1, 2): gAB,
        (1, 3): gAc,
        (2, 2): -t,
        (2, 3): gBc,
        (3, 3): gcc,
    }
    return 1.0 - h, first, second


PAIRS = [(p, q) for p in range(4) for q in range(p, 4)]


def derivatives(rho, A, B, c):
    kappa = 1.0 / cutoff_sq
    inv_r = lax.rsqrt(rho)
    tau = inv_r * inv_r
    cc = c * c
    e1 = lax.rsqrt(1.0 - (chi_shape * chi_shape) * cc)
    D1 = e1 * e1
    D2 = 1.0 / (1.0 - (chi_energy * chi_energy) * cc)
    AB = A * B
    norm = A * A + B * B
    twice_cab = 2.0 * c * AB
    prod_tau = AB * tau
    g, g1, g2 = anisotropy(chi_shape, D1, tau, A, B, c, norm, twice_cab, prod_tau)
    q, q1, q2 = anisotropy(chi_energy, D2, tau, A, B, c, norm, twice_cab, prod_tau)
    sigma = lax.rsqrt(g)
    root_g = g * sigma
    alpha = 0.5 * sigma * sigma * sigma
    s = 1.0 / (rho * inv_r - sigma + 1.0)
    s2 = s * s
    s6 = s2 * s2 * s2
    p = jnp.maximum(1.0 - kappa * rho, 0.0)
    inv_p = jnp.where(p > 0.0, 1.0 / p, 0.0)
    weight = (4.0 * well_depth) * e1 * (q * q) * (p * p * p) * s6
    w0 = weight * (s6 - 1.0)
    w1 = weight * s * (6.0 - 12.0 * s6)
    w2 = weight * s2 * (156.0 * s6 - 42.0)
    twice_inv_q = 2.0 / q
    L = [twice_inv_q * f for f in q1]
    lP = (-6.0 * kappa) * inv_p
    lK = (chi_shape * chi_shape) * c * D1
    lKK = (chi_shape * chi_shape) * D1 * (2.0 * D1 - 1.0)
    l = [L[0] + lP, L[1], L[2], L[3] + lK]
    G = [alpha * f for f in g1]
    R = [G[0] + inv_r, G[1], G[2], G[3]]
    half = [0.5 * f for f in L]
    bend = [3.0 * root_g * f for f in G]
    up = [w0 * l[k] + w1 * R[k] for k in range(4)]
    tp = [w1 * l[k] + w2 * R[k] for k in range(4)]
    w1a = w1 * alpha
    w0q = w0 * twice_inv_q
    out = []
    for a, b in PAIRS:
        value = up[a] * l[b] + tp[a] * R[b]
        value = value + w0q * q2[(a, b)] - w0 * (half[a] * L[b])
        value = value + w1a * g2[(a, b)] - w1 * (bend[a] * G[b])
        if (a, b) == (0, 0):
            value = value - w0 * (lP * lP) * (1.0 / 3.0) - w1 * (inv_r * tau)
        if (a, b) == (3, 3):
            value = value + w0 * lKK
        out.append(value)
    return up, out


def apply_pairs(d, u, v, dd, m, n, F, FF):
    S = dict(zip(PAIRS, FF))
    delta = (
        dot3(d, dd),
        dot3(u, dd) + dot3(d, m),
        dot3(v, dd) + dot3(d, n),
        dot3(v, m) + dot3(u, n),
    )
    dF = []
    for p in range(4):
        terms = [S[(min(p, q), max(p, q))] * delta[q] for q in range(4)]
        dF.append((terms[0] + terms[1]) + (terms[2] + terms[3]))
    Gd, Gu, Gv = [], [], []
    for k in range(3):
        Gd.append(
            (dF[0] * d[k] + F[0] * dd[k])
            + (dF[1] * u[k] + F[1] * m[k])
            + (dF[2] * v[k] + F[2] * n[k])
        )
        Gu.append((dF[1] * d[k] + F[1] * dd[k]) + (dF[3] * v[k] + F[3] * n[k]))
        Gv.append((dF[2] * d[k] + F[2] * dd[k]) + (dF[3] * u[k] + F[3] * m[k]))
    return Gd, Gu, Gv


def full(row):
    return jnp.broadcast_to(row, (CHUNK, LANES))


def rows_of(frame, vector):
    c = [frame[k : k + 1, :] for k in range(3)]
    u = [frame[3 + k : 4 + k, :] for k in range(3)]
    y = [vector[k : k + 1, :] for k in range(3)]
    w = [vector[3 + k : 4 + k, :] for k in range(3)]
    return c, u, y, list(cross3(w, u))


def put_columns(cols_ref, rows):
    pad = 16 - len(rows)
    block = jnp.concatenate(list(rows) + [jnp.zeros((pad, LANES), jnp.float32)], axis=0)
    cols_ref[...] = block.T


def gather_sums(sums_ref):
    return sums_ref[...].T


def column(block, p):
    return jnp.broadcast_to(block[:, p : p + 1], (CHUNK, LANES))


def merge_columns(values):
    lane = lax.broadcasted_iota(jnp.int32, (CHUNK, LANES), 1)
    out = jnp.zeros((CHUNK, LANES), jnp.float32)
    for k, value in enumerate(values):
        out = jnp.where(lane == k, jnp.sum(value, axis=1, keepdims=True), out)
    return out


def first_pass(slot, left, right, shift, cols_ref, sums_ref, kept_ref, own):
    cl, ul, yl, ml = left
    cr, ur, yr, nr = right
    put_columns(cols_ref, cl + ul + yl + ml)
    c_right = [full(cr[k] + shift[k]) for k in range(3)]
    v = [full(f) for f in ur]
    y_right = [full(f) for f in yr]
    n = [full(f) for f in nr]
    lane = lax.broadcasted_iota(jnp.int32, (CHUNK, LANES), 1)
    sub = lax.broadcasted_iota(jnp.int32, (CHUNK, LANES), 0)

    def chunk(i, acc):
        at = pl.multiple_of(i * CHUNK, CHUNK)
        block = cols_ref[pl.ds(at, CHUNK), :]
        d = [c_right[k] - column(block, k) for k in range(3)]
        u = [column(block, 3 + k) for k in range(3)]
        dd = [y_right[k] - column(block, 6 + k) for k in range(3)]
        m = [column(block, 9 + k) for k in range(3)]
        if own:
            d[2] = d[2] + jnp.where(sub + at == lane, 8.0, 0.0)
        A, B, c = dot3(d, u), dot3(d, v), dot3(u, v)
        F, FF = derivatives(dot3(d, d), A, B, c)
        if own:
            upper = sub + at < lane
            F = [jnp.where(upper, f, 0.0) for f in F]
            FF = [jnp.where(upper, f, 0.0) for f in FF]
        for k, value in enumerate(d + u + F + FF):
            kept_ref[slot, k, pl.ds(at, CHUNK), :] = value
        Gd, Gu, Gv = apply_pairs(d, u, v, dd, m, n, F, FF)
        fc = F[3] * c
        sums_ref[pl.ds(at, CHUNK), :] = merge_columns(Gd + Gu + [F[1] * A + fc])
        return tuple(a + g for a, g in zip(acc, Gd + Gv + [F[2] * B + fc]))

    zero = jnp.zeros((CHUNK, LANES), jnp.float32)
    acc = lax.fori_loop(0, LANES // CHUNK, chunk, (zero,) * 7)
    left_sums = gather_sums(sums_ref)
    left_curve = left_sums[6:7, :]
    right_rows = [jnp.sum(a, axis=0, keepdims=True) for a in acc]
    left_out, right_out = finish(left_sums, right_rows, left_curve, right_rows[6], ml, nr)
    return left_out, right_out, left_curve, right_rows[6]


def second_pass(slot, left, right, cols_ref, sums_ref, kept_ref, left_curve, right_curve):
    _, _, yl, ml = left
    _, ur, yr, nr = right
    put_columns(cols_ref, yl + ml)
    v = [full(f) for f in ur]
    y_right = [full(f) for f in yr]
    n = [full(f) for f in nr]

    def chunk(i, acc):
        at = pl.multiple_of(i * CHUNK, CHUNK)
        block = cols_ref[pl.ds(at, CHUNK), :]
        kept = [kept_ref[slot, k, pl.ds(at, CHUNK), :] for k in range(KEPT)]
        dd = [y_right[k] - column(block, k) for k in range(3)]
        m = [column(block, 3 + k) for k in range(3)]
        Gd, Gu, Gv = apply_pairs(kept[0:3], kept[3:6], v, dd, m, n, kept[6:10], kept[10:20])
        sums_ref[pl.ds(at, CHUNK), :] = merge_columns(Gd + Gu)
        return tuple(a + g for a, g in zip(acc, Gd + Gv))

    zero = jnp.zeros((CHUNK, LANES), jnp.float32)
    acc = lax.fori_loop(0, LANES // CHUNK, chunk, (zero,) * 6)
    left_sums = gather_sums(sums_ref)
    right_rows = [jnp.sum(a, axis=0, keepdims=True) for a in acc]
    return finish(left_sums, right_rows, left_curve, right_curve, ml, nr)


def finish(left_sums, right_rows, left_curve, right_curve, ml, nr):
    blank = jnp.zeros((2, LANES), jnp.float32)
    left_out = jnp.concatenate(
        [-left_sums[k : k + 1, :] for k in range(3)]
        + [left_sums[3 + k : 4 + k, :] - left_curve * ml[k] for k in range(3)]
        + [blank],
        axis=0,
    )
    right_out = jnp.concatenate(
        right_rows[0:3]
        + [right_rows[3 + k] - right_curve * nr[k] for k in range(3)]
        + [blank],
        axis=0,
    )
    return left_out, right_out


def triple_of(x, z):
    F = jnp.sum(x * x, axis=0, keepdims=True)
    some = F > 0.0
    a = jnp.where(some, jnp.sum(x * z, axis=0, keepdims=True) / jnp.where(some, F, 1.0), 0.0)
    rest = z - a * x
    return F, a, jnp.sum(rest * rest, axis=0, keepdims=True)


def merge_triples(F, a, R, axis):
    total = jnp.sum(F, axis=axis, keepdims=True)
    some = total > 0.0
    mean = jnp.where(some, jnp.sum(F * a, axis=axis, keepdims=True) / jnp.where(some, total, 1.0), 0.0)
    gap = a - mean
    return total, mean, jnp.sum(R + F * (gap * gap), axis=axis, keepdims=True)


def pack_triple(triple):
    return jnp.concatenate(list(triple) + [jnp.zeros((5, LANES), jnp.float32)], axis=0)


def unpack_triples(block):
    return block[:, 0, :], block[:, 1, :], block[:, 2, :]


def kernel(
    n_row, n_col,
    frame_ref, start_ref, list_ref, count_ref,
    coef_ref, mode_ref,
    row_frames, col_frames, row_starts, col_starts, row_images, col_images,
    row_in, col_in, row_in2, col_in2, row_out, col_out,
    tri_row, tri_col, tri_row2, tri_col2, tri_buf,
    image_buf, left_outs, right_outs, curves, kept_ref, cols_ref, sums_ref,
    send_sem, recv_sem,
):
    entries = list_ref.shape[0]
    r = lax.axis_index("row")
    c = lax.axis_index("col")
    total_entries = float(6 * LANES * n_row * n_col)
    zero3 = (0.0, 0.0, 0.0)

    def peer_col(k):
        return lax.rem(c + k, n_col)

    def peer_row(k):
        return lax.rem(r + k, n_row)

    def send(src, dst, phase, lane, device):
        pltpu.make_async_remote_copy(
            src_ref=src,
            dst_ref=dst,
            send_sem=send_sem.at[phase, lane],
            recv_sem=recv_sem.at[phase, lane],
            device_id=device,
            device_id_type=MESH,
        ).start()

    def all_wait(buf, n, sem):
        view = buf.at[pl.ds(0, n - 1)]
        pltpu.make_async_copy(view, view, sem).wait()

    barrier = pltpu.get_barrier_semaphore()

    @pl.loop(1, n_col)
    def _(k):
        pl.semaphore_signal(barrier, inc=1, device_id={"col": peer_col(k)}, device_id_type=MESH)

    @pl.loop(1, n_row)
    def _(k):
        pl.semaphore_signal(barrier, inc=1, device_id={"row": peer_row(k)}, device_id_type=MESH)

    frame = frame_ref[...]
    start = start_ref[...]
    mine = rows_of(frame, start)
    own1, own2, lc, rc = first_pass(entries, mine, mine, zero3, cols_ref, sums_ref, kept_ref, True)
    curves[entries, 0:1, :] = lc
    curves[entries, 1:2, :] = rc
    own_first = own1 + own2

    pl.semaphore_wait(barrier, n_row + n_col - 2)

    def spread(row_src, row_buf, col_src, col_buf, phase):
        @pl.loop(1, n_col)
        def _(k):
            send(row_src, row_buf.at[c], phase, 0, {"col": peer_col(k)})

        @pl.loop(1, n_row)
        def _(k):
            send(col_src, col_buf.at[r], phase, 1, {"row": peer_row(k)})

    spread(frame_ref, row_frames, frame_ref, col_frames, 0)
    spread(start_ref, row_starts, start_ref, col_starts, 1)
    row_frames[c] = frame
    col_frames[r] = frame
    row_starts[c] = start
    col_starts[r] = start
    all_wait(row_frames, n_col, recv_sem.at[0, 0])
    all_wait(col_frames, n_row, recv_sem.at[0, 1])
    all_wait(row_starts, n_col, recv_sem.at[1, 0])
    all_wait(col_starts, n_row, recv_sem.at[1, 1])

    period = (5.0, 5.0, 3.5 * (LANES // 16))

    def entry_rows(k, row_vectors, col_vectors):
        a = list_ref[k, 0]
        b = list_ref[k, 1]
        left = rows_of(row_frames[a], row_vectors[a])
        right = rows_of(col_frames[b], col_vectors[b])
        return left, right

    @pl.loop(0, entries)
    def _(k):
        left, right = entry_rows(k, row_starts, col_starts)
        shift = [list_ref[k, 2 + x].astype(jnp.float32) * period[x] for x in range(3)]
        lo, ro, lc, rc = first_pass(k, left, right, shift, cols_ref, sums_ref, kept_ref, False)
        left_outs[k] = lo
        right_outs[k] = ro
        curves[k, 0:1, :] = lc
        curves[k, 1:2, :] = rc

    used = count_ref[0, 0]

    def scatter(row_buf, col_buf, phase, own):
        lefts = [jnp.where(k < used, left_outs[k], 0.0) for k in range(entries)]
        rights = [jnp.where(k < used, right_outs[k], 0.0) for k in range(entries)]

        @pl.loop(0, n_col)
        def _(t):
            acc = jnp.zeros((8, LANES), jnp.float32)
            for k in range(entries):
                acc = acc + jnp.where(list_ref[k, 0] == t, lefts[k], 0.0)
            row_out[phase, t] = acc

        @pl.loop(0, n_row)
        def _(t):
            acc = jnp.zeros((8, LANES), jnp.float32)
            for k in range(entries):
                acc = acc + jnp.where(list_ref[k, 1] == t, rights[k], 0.0)
            col_out[phase, t] = acc

        @pl.loop(1, n_col)
        def _(k):
            t = peer_col(k)
            send(row_out.at[phase, t], row_buf.at[c], 2 + phase, 0, {"col": t})

        @pl.loop(1, n_row)
        def _(k):
            t = peer_row(k)
            send(col_out.at[phase, t], col_buf.at[r], 2 + phase, 1, {"row": t})

        row_buf[c] = row_out[phase, c]
        col_buf[r] = col_out[phase, r]
        all_wait(row_buf, n_col, recv_sem.at[2 + phase, 0])
        all_wait(col_buf, n_row, recv_sem.at[2 + phase, 1])
        total = own + jnp.sum(row_buf[...], axis=0) + jnp.sum(col_buf[...], axis=0)
        u = [frame[3 + k : 4 + k, :] for k in range(3)]
        turn = cross3(u, [total[3 + k : 4 + k, :] for k in range(3)])
        return jnp.concatenate([total[0:3, :]] + list(turn), axis=0)

    image = scatter(row_in, col_in, 0, own_first)

    image_buf[...] = image
    spread(image_buf, row_images, image_buf, col_images, 4)
    row_images[c] = image
    col_images[r] = image

    def scalars_out(triple, slot, buf, phase):
        tri_buf[slot] = pack_triple(triple)

        @pl.loop(1, n_row)
        def _(k):
            send(tri_buf.at[slot], buf.at[r], phase, 1, {"row": peer_row(k)})

        buf[r] = tri_buf[slot]

    def scalars_across(buf, slot, buf2, phase):
        all_wait(buf, n_row, recv_sem.at[phase, 1])
        triple = merge_triples(*unpack_triples(buf[...]), 0)
        tri_buf[slot] = pack_triple(triple)

        @pl.loop(1, n_col)
        def _(k):
            send(tri_buf.at[slot], buf2.at[c], phase, 0, {"col": peer_col(k)})

        buf2[c] = tri_buf[slot]

    def scalars_in(buf2, phase):
        all_wait(buf2, n_col, recv_sem.at[phase, 0])
        triple = merge_triples(*unpack_triples(buf2[...]), 0)
        return merge_triples(*triple, 1)

    scalars_out(triple_of(start, image), 0, tri_row, 5)

    mine = rows_of(frame, image)
    own1, own2 = second_pass(
        entries, mine, mine, cols_ref, sums_ref, kept_ref,
        curves[entries, 0:1, :], curves[entries, 1:2, :],
    )
    own_second = own1 + own2

    scalars_across(tri_row, 1, tri_col, 5)
    all_wait(row_images, n_col, recv_sem.at[4, 0])
    all_wait(col_images, n_row, recv_sem.at[4, 1])

    @pl.loop(0, entries)
    def _(k):
        left, right = entry_rows(k, row_images, col_images)
        lo, ro = second_pass(
            k, left, right, cols_ref, sums_ref, kept_ref, curves[k, 0:1, :], curves[k, 1:2, :]
        )
        left_outs[k] = lo
        right_outs[k] = ro

    image2 = scatter(row_in2, col_in2, 1, own_second)

    F, a, R = scalars_in(tri_col, 5)
    inv_n0 = lax.rsqrt(F / total_entries + norm_eps)
    alpha1 = (a * F) * (inv_n0 * inv_n0) / total_entries
    gap = a - alpha1
    beta1 = jnp.sqrt((R + gap * gap * F) * (inv_n0 * inv_n0) / total_entries + norm_eps)
    scale = inv_n0 / beta1
    second = (image - alpha1 * start) * scale
    image3 = (image2 - alpha1 * image) * scale - (beta1 * inv_n0) * start

    scalars_out(triple_of(second, image3), 2, tri_row2, 6)
    scalars_across(tri_row2, 3, tri_col2, 6)
    F, a, R = scalars_in(tri_col2, 6)
    alpha2 = (a * F) / total_entries
    gap = a - alpha2
    beta2 = jnp.sqrt((R + gap * gap * F) / total_entries + norm_eps)
    mode_ref[...] = (image3 - alpha2 * second) / beta2
    coef_ref[0] = alpha1[0, 0]
    coef_ref[1] = beta1[0, 0]
    coef_ref[2] = alpha2[0, 0]
    coef_ref[3] = beta2[0, 0]

    for phase, row_buf, col_buf in (
        (0, row_frames, col_frames),
        (1, row_starts, col_starts),
        (2, row_in, col_in),
        (3, row_in2, col_in2),
        (4, row_images, col_images),
        (5, tri_col, tri_row),
        (6, tri_col2, tri_row2),
    ):
        all_wait(row_buf, n_col, send_sem.at[phase, 0])
        all_wait(col_buf, n_row, send_sem.at[phase, 1])


def solution(mesh):
    n_row, n_col = mesh.shape["row"], mesh.shape["col"]

    def local(config, start, tile_list, tile_count):
        entries = tile_list.shape[2]
        f32 = jnp.float32

        def vm(*shape):
            return pltpu.VMEM(shape, f32)

        scratch = [
            vm(n_col, 6, LANES), vm(n_row, 6, LANES),
            vm(n_col, 6, LANES), vm(n_row, 6, LANES),
            vm(n_col, 6, LANES), vm(n_row, 6, LANES),
            vm(n_col, 8, LANES), vm(n_row, 8, LANES),
            vm(n_col, 8, LANES), vm(n_row, 8, LANES),
            vm(2, n_col, 8, LANES), vm(2, n_row, 8, LANES),
            vm(n_row, 8, LANES), vm(n_col, 8, LANES),
            vm(n_row, 8, LANES), vm(n_col, 8, LANES),
            vm(4, 8, LANES),
            vm(6, LANES),
            vm(entries, 8, LANES), vm(entries, 8, LANES),
            vm(entries + 1, 8, LANES),
            vm(entries + 1, KEPT, LANES, LANES),
            vm(LANES, 16),
            vm(LANES, LANES),
            pltpu.SemaphoreType.DMA((7, 2)),
            pltpu.SemaphoreType.DMA((7, 2)),
        ]
        return pl.pallas_call(
            functools.partial(kernel, n_row, n_col),
            out_shape=(
                jax.ShapeDtypeStruct((4,), f32),
                jax.ShapeDtypeStruct((6, LANES), f32),
            ),
            in_specs=[
                pl.BlockSpec(memory_space=pltpu.VMEM),
                pl.BlockSpec(memory_space=pltpu.VMEM),
                pl.BlockSpec(memory_space=pltpu.SMEM),
                pl.BlockSpec(memory_space=pltpu.SMEM),
            ],
            out_specs=(
                pl.BlockSpec(memory_space=pltpu.SMEM),
                pl.BlockSpec(memory_space=pltpu.VMEM),
            ),
            scratch_shapes=scratch,
            compiler_params=pltpu.CompilerParams(collective_id=0, has_side_effects=True),
        )(config, start, tile_list.reshape(entries, 5), tile_count)

    placed = (
        P(None, ("row", "col")),
        P(None, ("row", "col")),
        P("row", "col", None, None),
        P("row", "col"),
    )
    return jax.shard_map(
        local, mesh=mesh, in_specs=placed, out_specs=(P(), P(None, ("row", "col"))), check_vma=False
    )
```

time: 1340 us -> 121 us (0.09)
  blocking collectives: 650 us -> 0 us
  waiting for transfers between devices: 631 us -> 0 us
  Pallas kernels: 0 us -> 117 us
  other arithmetic: 20.8 us -> 0 us
  between operations: 17.7 us -> 1.29 us
    psum x2 -> x0, waiting for transfers between devices: 631 us -> none  [apply_hessian(): lax.psum(layout.reshape(6, row_devices * col_devices * member), ('row', '...]
    psum x5 -> x0, blocking collectives: 477 us -> none  [mean_one(): return lax.psum(jnp.sum(values), ('row', 'col')) / total_entries]
    all_gather x6 -> x0, blocking collectives: 173 us -> none  [the longest x2 59 us: apply_hessian(): row_vectors = lax.all_gather(vector, 'col', axis=1, tiled=True)]
    pallas_call x0 -> x1, Pallas kernels: none -> 117 us  [local(): pl.pallas_call(functools.partial(kernel, n_row, n_col), out_shape=(jax.Sh...]
  transfers between devices with their start and end apart: 2 -> 0, of which waited for: 2 -> 0; matrix products, arithmetic and copies ran while one was open for 0% -> 0% of each run, Pallas kernels for 0% -> 0%
where the time goes in v1:
time: 121 us
  Pallas kernels  117 us (97%)
  local copies, waits for them, and re-layouts  3.13 us (3%)
  between operations  1.29 us (1%)
    pallas_call x1, Pallas kernels, local(): pl.pallas_call(functools.partial(kernel, n_row, n_col), out_shape=(jax.Sh...  117 us
    unnamed x5, local copies, waits for them, and re-layouts  3.13 us

profile of v1, /device:TPU:1, one launch (start us, length us, event | category | flops | bytes accessed | tf_op | source)
XLA Modules:
  0.0 121.0 jit_solution(4859709725524948468)
XLA Ops:
  1.3 1.4 %copy.6 = s32[1,1,8,5]{3,2,1,0:T(8,128)} copy(s32[1,1,8,5]{2,1,3,0:T(1,128)} %param.6) | data formatting | bytes 320 | tf_op args[2]
  2.6 116.6 %shard_map.59 = (f32[4]{0:T(128)}, f32[6,128]{1,0:T(8,128)}) custom-call(f32[6,128]{1,0:T(8,128)} %frame_ref.1, f32[6,128]{1,0:T(8,128)} %start_ref.1, s32[8,5]{1,0:T(8,128)} %bitcast.1, s32[1,1]{1,0:T(1,128)S(6)} %copy.9.count_ref), custom_call_target="tpu_custom_call" | custom-call | tf_op jit(solution)/shard_map/pallas_call | solution.py:539
  119.2 0.0 copy-start
  119.2 1.2 copy.10
  120.4 0.0 copy-done
  120.4 0.6 copy.11
Async XLA Ops:
  119.2 1.2 copy-start

commit v2 on v1

--- a/solution.py
+++ b/solution.py
@@ -17,6 +17,8 @@
 LANES = 128
 CHUNK = 8
 KEPT = 20
+UNROLL_FIRST = 4
+UNROLL_SECOND = 4
 
 
 def dot3(a, b):
@@ -98,19 +100,21 @@
     l = [L[0] + lP, L[1], L[2], L[3] + lK]
     G = [alpha * f for f in g1]
     R = [G[0] + inv_r, G[1], G[2], G[3]]
-    half = [0.5 * f for f in L]
-    bend = [3.0 * root_g * f for f in G]
     up = [w0 * l[k] + w1 * R[k] for k in range(4)]
     tp = [w1 * l[k] + w2 * R[k] for k in range(4)]
+    w0h = 0.5 * w0
+    w1b = (3.0 * root_g) * w1
+    upp = [up[k] - w0h * L[k] for k in range(4)]
+    tpp = [tp[k] - w1b * G[k] for k in range(4)]
     w1a = w1 * alpha
     w0q = w0 * twice_inv_q
     out = []
     for a, b in PAIRS:
-        value = up[a] * l[b] + tp[a] * R[b]
-        value = value + w0q * q2[(a, b)] - w0 * (half[a] * L[b])
-        value = value + w1a * g2[(a, b)] - w1 * (bend[a] * G[b])
+        value = (upp[a] * L[b] + tpp[a] * G[b]) + (w0q * q2[(a, b)] + w1a * g2[(a, b)])
+        if b == 3:
+            value = value + up[a] * lK
         if (a, b) == (0, 0):
-            value = value - w0 * (lP * lP) * (1.0 / 3.0) - w1 * (inv_r * tau)
+            value = value + (up[0] - w0 * lP * (1.0 / 3.0)) * lP + (tp[0] - w1 * tau) * inv_r
         if (a, b) == (3, 3):
             value = value + w0 * lKK
         out.append(value)
@@ -145,6 +149,16 @@
     return jnp.broadcast_to(row, (CHUNK, LANES))
 
 
+def skew(row):
+    return pltpu.roll(full(row), 0, 1, stride=1, stride_axis=0)
+
+
+def unskew_sum(a):
+    for rows in (4, 2, 1):
+        a = a[0:rows, :] + pltpu.roll(a[rows : 2 * rows, :], LANES - rows, 1)
+    return a
+
+
 def rows_of(frame, vector):
     c = [frame[k : k + 1, :] for k in range(3)]
     u = [frame[3 + k : 4 + k, :] for k in range(3)]
@@ -153,110 +167,175 @@
     return c, u, y, list(cross3(w, u))
 
 
-def put_columns(cols_ref, rows):
-    pad = 16 - len(rows)
-    block = jnp.concatenate(list(rows) + [jnp.zeros((pad, LANES), jnp.float32)], axis=0)
-    cols_ref[...] = block.T
-
-
-def gather_sums(sums_ref):
-    return sums_ref[...].T
-
-
-def column(block, p):
-    return jnp.broadcast_to(block[:, p : p + 1], (CHUNK, LANES))
-
-
-def merge_columns(values):
-    lane = lax.broadcasted_iota(jnp.int32, (CHUNK, LANES), 1)
-    out = jnp.zeros((CHUNK, LANES), jnp.float32)
-    for k, value in enumerate(values):
-        out = jnp.where(lane == k, jnp.sum(value, axis=1, keepdims=True), out)
-    return out
-
-
-def first_pass(slot, left, right, shift, cols_ref, sums_ref, kept_ref, own):
+def place_tile(slot, left, right, shift, bufs):
+    left_ref, right_ref = bufs[0], bufs[1]
     cl, ul, yl, ml = left
     cr, ur, yr, nr = right
-    put_columns(cols_ref, cl + ul + yl + ml)
-    c_right = [full(cr[k] + shift[k]) for k in range(3)]
-    v = [full(f) for f in ur]
-    y_right = [full(f) for f in yr]
-    n = [full(f) for f in nr]
+    if shift is not None:
+        for k in range(3):
+            left_ref[slot, k] = full(cl[k])
+            left_ref[slot, 3 + k] = full(ul[k])
+            right_ref[slot, 6 + k] = skew(cr[k] + shift[k])
+            right_ref[slot, 9 + k] = skew(ur[k])
+    for k in range(3):
+        left_ref[slot, 6 + k] = full(yl[k])
+        left_ref[slot, 9 + k] = full(ml[k])
+        right_ref[slot, k] = skew(yr[k])
+        right_ref[slot, 3 + k] = skew(nr[k])
+
+
+def sweep(step, bufs, slot0, slots, unroll, turned, width):
+    _, right_ref, turn_ref, raw_ref, left_sums, right_sums, _ = bufs
+    chunks = LANES // CHUNK
+    groups = chunks // unroll
+
+    def turn_rows(trip):
+        slot = slot0 + trip // groups
+        side = lax.rem(trip, 2)
+        for s in range(unroll):
+            by = (lax.rem(trip, groups) * unroll + s) * CHUNK
+            for k in range(turned):
+                turn_ref[side, s, k] = pltpu.roll(right_ref[slot, k], by, 1)
+
+    def turn_back(trip):
+        slot = slot0 + trip // groups
+        group = lax.rem(trip, groups)
+        side = lax.rem(trip, 2)
+        for k in range(width):
+            total = None
+            for s in range(unroll):
+                by = lax.rem(LANES - (group * unroll + s) * CHUNK, LANES)
+                part = pltpu.roll(raw_ref[side, s, k], by, 1)
+                total = part if total is None else total + part
+            right_sums[slot, group, k] = total
+
+    def body(trip):
+        slot = slot0 + trip // groups
+        group = lax.rem(trip, groups)
+        side = lax.rem(trip, 2)
+        sums = None
+        for s in range(unroll):
+            left_terms, right_terms = step(slot, group * unroll + s, side, s)
+            for k in range(width):
+                raw_ref[side, s, k] = right_terms[k]
+            sums = left_terms if sums is None else [a + b for a, b in zip(sums, left_terms)]
+        for k in range(width):
+            left_sums[slot, group, k] = sums[k]
+
+    trips = slots * groups
+    turn_rows(0)
+
+    def first(trip, carry):
+        turn_rows(trip + 1)
+        body(trip)
+        return carry
+
+    def later(trip, carry):
+        turn_back(trip - 1)
+        turn_rows(trip + 1)
+        body(trip)
+        return carry
+
+    first(0, 0)
+    lax.fori_loop(1, trips - 1, later, 0)
+    turn_back(trips - 2)
+    body(trips - 1)
+    turn_back(trips - 1)
+
+
+def collect(slot, bufs, groups, width):
+    left_sums, right_sums = bufs[4], bufs[5]
+    left, right = [], []
+    for k in range(width):
+        a, b = left_sums[slot, 0, k], right_sums[slot, 0, k]
+        for g in range(1, groups):
+            a = a + left_sums[slot, g, k]
+            b = b + right_sums[slot, g, k]
+        left.append(jnp.sum(a, axis=0, keepdims=True))
+        right.append(unskew_sum(b))
+    return left, right
+
+
+def first_sweep(bufs, slot0, slots, own):
+    left_ref, _, turn_ref, _, _, _, kept_ref = bufs
     lane = lax.broadcasted_iota(jnp.int32, (CHUNK, LANES), 1)
     sub = lax.broadcasted_iota(jnp.int32, (CHUNK, LANES), 0)
 
-    def chunk(i, acc):
-        at = pl.multiple_of(i * CHUNK, CHUNK)
-        block = cols_ref[pl.ds(at, CHUNK), :]
-        d = [c_right[k] - column(block, k) for k in range(3)]
-        u = [column(block, 3 + k) for k in range(3)]
-        dd = [y_right[k] - column(block, 6 + k) for k in range(3)]
-        m = [column(block, 9 + k) for k in range(3)]
+    def step(slot, t, side, s):
+        left = [left_ref[slot, k] for k in range(12)]
+        right = [turn_ref[side, s, k] for k in range(12)]
+        d = [right[6 + k] - left[k] for k in range(3)]
+        u, v = left[3:6], right[9:12]
+        dd = [right[k] - left[6 + k] for k in range(3)]
+        m, n = left[9:12], right[3:6]
         if own:
-            d[2] = d[2] + jnp.where(sub + at == lane, 8.0, 0.0)
+            gap = sub + t * CHUNK
+            d[2] = d[2] + jnp.where(gap == 0, 8.0, 0.0)
         A, B, c = dot3(d, u), dot3(d, v), dot3(u, v)
         F, FF = derivatives(dot3(d, d), A, B, c)
         if own:
-            upper = sub + at < lane
-            F = [jnp.where(upper, f, 0.0) for f in F]
-            FF = [jnp.where(upper, f, 0.0) for f in FF]
-        for k, value in enumerate(d + u + F + FF):
-            kept_ref[slot, k, pl.ds(at, CHUNK), :] = value
+            once = (gap > 0) & (lane >= gap)
+            F = [jnp.where(once, f, 0.0) for f in F]
+            FF = [jnp.where(once, f, 0.0) for f in FF]
+        for k, value in enumerate(d + v + F + FF):
+            kept_ref[slot, t, k] = value
         Gd, Gu, Gv = apply_pairs(d, u, v, dd, m, n, F, FF)
         fc = F[3] * c
-        sums_ref[pl.ds(at, CHUNK), :] = merge_columns(Gd + Gu + [F[1] * A + fc])
-        return tuple(a + g for a, g in zip(acc, Gd + Gv + [F[2] * B + fc]))
-
-    zero = jnp.zeros((CHUNK, LANES), jnp.float32)
-    acc = lax.fori_loop(0, LANES // CHUNK, chunk, (zero,) * 7)
-    left_sums = gather_sums(sums_ref)
-    left_curve = left_sums[6:7, :]
-    right_rows = [jnp.sum(a, axis=0, keepdims=True) for a in acc]
-    left_out, right_out = finish(left_sums, right_rows, left_curve, right_rows[6], ml, nr)
-    return left_out, right_out, left_curve, right_rows[6]
-
-
-def second_pass(slot, left, right, cols_ref, sums_ref, kept_ref, left_curve, right_curve):
-    _, _, yl, ml = left
-    _, ur, yr, nr = right
-    put_columns(cols_ref, yl + ml)
-    v = [full(f) for f in ur]
-    y_right = [full(f) for f in yr]
-    n = [full(f) for f in nr]
-
-    def chunk(i, acc):
-        at = pl.multiple_of(i * CHUNK, CHUNK)
-        block = cols_ref[pl.ds(at, CHUNK), :]
-        kept = [kept_ref[slot, k, pl.ds(at, CHUNK), :] for k in range(KEPT)]
-        dd = [y_right[k] - column(block, k) for k in range(3)]
-        m = [column(block, 3 + k) for k in range(3)]
-        Gd, Gu, Gv = apply_pairs(kept[0:3], kept[3:6], v, dd, m, n, kept[6:10], kept[10:20])
-        sums_ref[pl.ds(at, CHUNK), :] = merge_columns(Gd + Gu)
-        return tuple(a + g for a, g in zip(acc, Gd + Gv))
-
-    zero = jnp.zeros((CHUNK, LANES), jnp.float32)
-    acc = lax.fori_loop(0, LANES // CHUNK, chunk, (zero,) * 6)
-    left_sums = gather_sums(sums_ref)
-    right_rows = [jnp.sum(a, axis=0, keepdims=True) for a in acc]
-    return finish(left_sums, right_rows, left_curve, right_curve, ml, nr)
-
-
-def finish(left_sums, right_rows, left_curve, right_curve, ml, nr):
+        return Gd + Gu + [F[1] * A + fc], Gd + Gv + [F[2] * B + fc]
+
+    sweep(step, bufs, slot0, slots, UNROLL_FIRST, 12, 7)
+
+
+def second_sweep(bufs, slot0, slots):
+    left_ref, _, turn_ref, _, _, _, kept_ref = bufs
+
+    def step(slot, t, side, s):
+        u, yl, m = ([left_ref[slot, first + k] for k in range(3)] for first in (3, 6, 9))
+        right = [turn_ref[side, s, k] for k in range(6)]
+        kept = [kept_ref[slot, t, k] for k in range(KEPT)]
+        dd = [right[k] - yl[k] for k in range(3)]
+        Gd, Gu, Gv = apply_pairs(kept[0:3], u, kept[3:6], dd, m, right[3:6], kept[6:10], kept[10:20])
+        return Gd + Gu, Gd + Gv
+
+    sweep(step, bufs, slot0, slots, UNROLL_SECOND, 6, 6)
+
+
+def finish(left, right, left_curve, right_curve, ml, nr):
     blank = jnp.zeros((2, LANES), jnp.float32)
     left_out = jnp.concatenate(
-        [-left_sums[k : k + 1, :] for k in range(3)]
-        + [left_sums[3 + k : 4 + k, :] - left_curve * ml[k] for k in range(3)]
-        + [blank],
+        [-left[k] for k in range(3)] + [left[3 + k] - left_curve * ml[k] for k in range(3)] + [blank],
         axis=0,
     )
     right_out = jnp.concatenate(
-        right_rows[0:3]
-        + [right_rows[3 + k] - right_curve * nr[k] for k in range(3)]
-        + [blank],
+        right[0:3] + [right[3 + k] - right_curve * nr[k] for k in range(3)] + [blank],
         axis=0,
     )
     return left_out, right_out
+
+
+def first_product(bufs, slot0, tiles, shifts, curves, own):
+    for k, (left, right) in enumerate(tiles):
+        place_tile(slot0 + k, left, right, shifts[k], bufs)
+    first_sweep(bufs, slot0, len(tiles), own)
+    out = []
+    for k, (left, right) in enumerate(tiles):
+        sl, sr = collect(slot0 + k, bufs, LANES // CHUNK // UNROLL_FIRST, 7)
+        curves[slot0 + k, 0:1, :] = sl[6]
+        curves[slot0 + k, 1:2, :] = sr[6]
+        out.append(finish(sl, sr, sl[6], sr[6], left[3], right[3]))
+    return out
+
+
+def second_product(bufs, slot0, tiles, curves):
+    for k, (left, right) in enumerate(tiles):
+        place_tile(slot0 + k, left, right, None, bufs)
+    second_sweep(bufs, slot0, len(tiles))
+    out = []
+    for k, (left, right) in enumerate(tiles):
+        sl, sr = collect(slot0 + k, bufs, LANES // CHUNK // UNROLL_SECOND, 6)
+        at = slot0 + k
+        out.append(finish(sl, sr, curves[at, 0:1, :], curves[at, 1:2, :], left[3], right[3]))
+    return out
 
 
 def triple_of(x, z):
@@ -290,10 +369,11 @@
     row_frames, col_frames, row_starts, col_starts, row_images, col_images,
     row_in, col_in, row_in2, col_in2, row_out, col_out,
     tri_row, tri_col, tri_row2, tri_col2, tri_buf,
-    image_buf, left_outs, right_outs, curves, kept_ref, cols_ref, sums_ref,
+    image_buf, curves, left_ref, right_ref, turn_ref, raw_ref, left_sums, right_sums, kept_ref,
     send_sem, recv_sem,
 ):
     entries = list_ref.shape[0]
+    bufs = (left_ref, right_ref, turn_ref, raw_ref, left_sums, right_sums, kept_ref)
     r = lax.axis_index("row")
     c = lax.axis_index("col")
     total_entries = float(6 * LANES * n_row * n_col)
@@ -332,9 +412,7 @@
     frame = frame_ref[...]
     start = start_ref[...]
     mine = rows_of(frame, start)
-    own1, own2, lc, rc = first_pass(entries, mine, mine, zero3, cols_ref, sums_ref, kept_ref, True)
-    curves[entries, 0:1, :] = lc
-    curves[entries, 1:2, :] = rc
+    ((own1, own2),) = first_product(bufs, entries, [(mine, mine)], [zero3], curves, True)
     own_first = own1 + own2
 
     pl.semaphore_wait(barrier, n_row + n_col - 2)
@@ -368,21 +446,17 @@
         right = rows_of(col_frames[b], col_vectors[b])
         return left, right
 
-    @pl.loop(0, entries)
-    def _(k):
-        left, right = entry_rows(k, row_starts, col_starts)
-        shift = [list_ref[k, 2 + x].astype(jnp.float32) * period[x] for x in range(3)]
-        lo, ro, lc, rc = first_pass(k, left, right, shift, cols_ref, sums_ref, kept_ref, False)
-        left_outs[k] = lo
-        right_outs[k] = ro
-        curves[k, 0:1, :] = lc
-        curves[k, 1:2, :] = rc
+    tiles = [entry_rows(k, row_starts, col_starts) for k in range(entries)]
+    shifts = [
+        [list_ref[k, 2 + x].astype(jnp.float32) * period[x] for x in range(3)] for k in range(entries)
+    ]
+    outs = first_product(bufs, 0, tiles, shifts, curves, False)
 
     used = count_ref[0, 0]
 
-    def scatter(row_buf, col_buf, phase, own):
-        lefts = [jnp.where(k < used, left_outs[k], 0.0) for k in range(entries)]
-        rights = [jnp.where(k < used, right_outs[k], 0.0) for k in range(entries)]
+    def scatter(row_buf, col_buf, phase, own, outs):
+        lefts = [jnp.where(k < used, outs[k][0], 0.0) for k in range(entries)]
+        rights = [jnp.where(k < used, outs[k][1], 0.0) for k in range(entries)]
 
         @pl.loop(0, n_col)
         def _(t):
@@ -414,10 +488,10 @@
         all_wait(col_buf, n_row, recv_sem.at[2 + phase, 1])
         total = own + jnp.sum(row_buf[...], axis=0) + jnp.sum(col_buf[...], axis=0)
         u = [frame[3 + k : 4 + k, :] for k in range(3)]
-        turn = cross3(u, [total[3 + k : 4 + k, :] for k in range(3)])
-        return jnp.concatenate([total[0:3, :]] + list(turn), axis=0)
-
-    image = scatter(row_in, col_in, 0, own_first)
+        twist = cross3(u, [total[3 + k : 4 + k, :] for k in range(3)])
+        return jnp.concatenate([total[0:3, :]] + list(twist), axis=0)
+
+    image = scatter(row_in, col_in, 0, own_first, outs)
 
     image_buf[...] = image
     spread(image_buf, row_images, image_buf, col_images, 4)
@@ -452,26 +526,17 @@
     scalars_out(triple_of(start, image), 0, tri_row, 5)
 
     mine = rows_of(frame, image)
-    own1, own2 = second_pass(
-        entries, mine, mine, cols_ref, sums_ref, kept_ref,
-        curves[entries, 0:1, :], curves[entries, 1:2, :],
-    )
+    ((own1, own2),) = second_product(bufs, entries, [(mine, mine)], curves)
     own_second = own1 + own2
 
     scalars_across(tri_row, 1, tri_col, 5)
     all_wait(row_images, n_col, recv_sem.at[4, 0])
     all_wait(col_images, n_row, recv_sem.at[4, 1])
 
-    @pl.loop(0, entries)
-    def _(k):
-        left, right = entry_rows(k, row_images, col_images)
-        lo, ro = second_pass(
-            k, left, right, cols_ref, sums_ref, kept_ref, curves[k, 0:1, :], curves[k, 1:2, :]
-        )
-        left_outs[k] = lo
-        right_outs[k] = ro
-
-    image2 = scatter(row_in2, col_in2, 1, own_second)
+    tiles = [entry_rows(k, row_images, col_images) for k in range(entries)]
+    outs = second_product(bufs, 0, tiles, curves)
+
+    image2 = scatter(row_in2, col_in2, 1, own_second, outs)
 
     F, a, R = scalars_in(tri_col, 5)
     inv_n0 = lax.rsqrt(F / total_entries + norm_eps)
@@ -513,6 +578,7 @@
     def local(config, start, tile_list, tile_count):
         entries = tile_list.shape[2]
         f32 = jnp.float32
+        unroll = max(UNROLL_FIRST, UNROLL_SECOND)
 
         def vm(*shape):
             return pltpu.VMEM(shape, f32)
@@ -528,11 +594,11 @@
             vm(n_row, 8, LANES), vm(n_col, 8, LANES),
             vm(4, 8, LANES),
             vm(6, LANES),
-            vm(entries, 8, LANES), vm(entries, 8, LANES),
             vm(entries + 1, 8, LANES),
-            vm(entries + 1, KEPT, LANES, LANES),
-            vm(LANES, 16),
-            vm(LANES, LANES),
+            vm(entries + 1, 12, CHUNK, LANES), vm(entries + 1, 12, CHUNK, LANES),
+            vm(2, unroll, 12, CHUNK, LANES), vm(2, unroll, 7, CHUNK, LANES),
+            vm(entries + 1, LANES // CHUNK, 7, CHUNK, LANES), vm(entries + 1, LANES // CHUNK, 7, CHUNK, LANES),
+            vm(entries + 1, LANES // CHUNK, KEPT, CHUNK, LANES),
             pltpu.SemaphoreType.DMA((7, 2)),
             pltpu.SemaphoreType.DMA((7, 2)),
         ]

time: 121 us -> 86.3 us (0.71)
  Pallas kernels: 117 us -> 81.6 us
    pallas_call x1, Pallas kernels: 117 us -> 81.6 us  [local(): pl.pallas_call(functools.partial(kernel, n_row, n_col), out_shape=(jax.Sh...]
where the time goes in v2:
time: 86.3 us; the launch traced here: 86 us
  Pallas kernels  81.6 us (95%)
  local copies, waits for them, and re-layouts  3.13 us (4%)
  between operations  1.29 us (1%)
    pallas_call x1, Pallas kernels, local(): pl.pallas_call(functools.partial(kernel, n_row, n_col), out_shape=(jax.Sh...  81.6 us
    unnamed x5, local copies, waits for them, and re-layouts  3.13 us

profile of v2, /device:TPU:1, one launch (start us, length us, event | category | flops | bytes accessed | tf_op | source)
XLA Modules:
  0.0 86.0 jit_solution(15272586528974302522)
XLA Ops:
  1.3 1.4 %copy.6 = s32[1,1,8,5]{3,2,1,0:T(8,128)} copy(s32[1,1,8,5]{2,1,3,0:T(1,128)} %param.6) | data formatting | bytes 320 | tf_op args[2]
  2.6 81.6 %shard_map.59 = (f32[4]{0:T(128)}, f32[6,128]{1,0:T(8,128)}) custom-call(f32[6,128]{1,0:T(8,128)} %frame_ref.1, f32[6,128]{1,0:T(8,128)} %start_ref.1, s32[8,5]{1,0:T(8,128)} %bitcast.1, s32[1,1]{1,0:T(1,128)S(6)} %copy.9.count_ref), custom_call_target="tpu_custom_call" | custom-call | tf_op jit(solution)/shard_map/pallas_call | solution.py:605
  84.3 0.0 copy-start
  84.3 1.2 %copy.10 = f32[4]{0:T(128)} copy(f32[4]{0:T(128)} %get-tuple-element.4) | data formatting | bytes 32
  85.4 0.0 copy-done
  85.5 0.6 copy.11
Async XLA Ops:
  84.3 1.2 %copy-start = (f32[6,128]{1,0:T(8,128)S(1)}, f32[6,128]{1,0:T(8,128)}, u32[]{:S(2)}) copy-start(f32[6,128]{1,0:T(8,128)} %get-tuple-element.5) | copy-start | bytes 9220

commit v3 on v2

--- a/solution.py
+++ b/solution.py
@@ -153,10 +153,11 @@
     return pltpu.roll(full(row), 0, 1, stride=1, stride_axis=0)
 
 
-def unskew_sum(a):
+def unskew_sums(blocks):
     for rows in (4, 2, 1):
-        a = a[0:rows, :] + pltpu.roll(a[rows : 2 * rows, :], LANES - rows, 1)
-    return a
+        turned = [pltpu.roll(a[rows : 2 * rows, :], LANES - rows, 1) for a in blocks]
+        blocks = [a[0:rows, :] + b for a, b in zip(blocks, turned)]
+    return blocks
 
 
 def rows_of(frame, vector):
@@ -243,17 +244,23 @@
     turn_back(trips - 1)
 
 
-def collect(slot, bufs, groups, width):
+def collect(slot0, slots, bufs, groups, width):
     left_sums, right_sums = bufs[4], bufs[5]
-    left, right = [], []
-    for k in range(width):
-        a, b = left_sums[slot, 0, k], right_sums[slot, 0, k]
-        for g in range(1, groups):
-            a = a + left_sums[slot, g, k]
-            b = b + right_sums[slot, g, k]
-        left.append(jnp.sum(a, axis=0, keepdims=True))
-        right.append(unskew_sum(b))
-    return left, right
+
+    def joined(ref):
+        out = []
+        for slot in range(slot0, slot0 + slots):
+            for k in range(width):
+                parts = [ref[slot, g, k] for g in range(groups)]
+                while len(parts) > 1:
+                    parts = [a + b for a, b in zip(parts[0::2], parts[1::2])]
+                out.append(parts[0])
+        return out
+
+    right = unskew_sums(joined(right_sums))
+    left = [jnp.sum(a, axis=0, keepdims=True) for a in joined(left_sums)]
+    cut = lambda rows: [rows[k * width : (k + 1) * width] for k in range(slots)]
+    return list(zip(cut(left), cut(right)))
 
 
 def first_sweep(bufs, slot0, slots, own):
@@ -318,8 +325,9 @@
         place_tile(slot0 + k, left, right, shifts[k], bufs)
     first_sweep(bufs, slot0, len(tiles), own)
     out = []
+    sums = collect(slot0, len(tiles), bufs, LANES // CHUNK // UNROLL_FIRST, 7)
     for k, (left, right) in enumerate(tiles):
-        sl, sr = collect(slot0 + k, bufs, LANES // CHUNK // UNROLL_FIRST, 7)
+        sl, sr = sums[k]
         curves[slot0 + k, 0:1, :] = sl[6]
         curves[slot0 + k, 1:2, :] = sr[6]
         out.append(finish(sl, sr, sl[6], sr[6], left[3], right[3]))
@@ -331,8 +339,9 @@
         place_tile(slot0 + k, left, right, None, bufs)
     second_sweep(bufs, slot0, len(tiles))
     out = []
+    sums = collect(slot0, len(tiles), bufs, LANES // CHUNK // UNROLL_SECOND, 6)
     for k, (left, right) in enumerate(tiles):
-        sl, sr = collect(slot0 + k, bufs, LANES // CHUNK // UNROLL_SECOND, 6)
+        sl, sr = sums[k]
         at = slot0 + k
         out.append(finish(sl, sr, curves[at, 0:1, :], curves[at, 1:2, :], left[3], right[3]))
     return out
@@ -355,7 +364,7 @@
 
 
 def pack_triple(triple):
-    return jnp.concatenate(list(triple) + [jnp.zeros((5, LANES), jnp.float32)], axis=0)
+    return jnp.concatenate(list(triple), axis=0)
 
 
 def unpack_triples(block):
@@ -366,24 +375,40 @@
     n_row, n_col,
     frame_ref, start_ref, list_ref, count_ref,
     coef_ref, mode_ref,
-    row_frames, col_frames, row_starts, col_starts, row_images, col_images,
+    row_frames, col_frames, row_images, col_images,
     row_in, col_in, row_in2, col_in2, row_out, col_out,
     tri_row, tri_col, tri_row2, tri_col2, tri_buf,
-    image_buf, curves, left_ref, right_ref, turn_ref, raw_ref, left_sums, right_sums, kept_ref,
+    pack_buf, image_buf, curves, left_ref, right_ref, turn_ref, raw_ref, left_sums, right_sums, kept_ref,
     send_sem, recv_sem,
 ):
-    entries = list_ref.shape[0]
+    entries = list_ref.shape[2]
+    entry = [[list_ref[x, 0, k] for x in range(5)] for k in range(entries)]
     bufs = (left_ref, right_ref, turn_ref, raw_ref, left_sums, right_sums, kept_ref)
     r = lax.axis_index("row")
     c = lax.axis_index("col")
     total_entries = float(6 * LANES * n_row * n_col)
     zero3 = (0.0, 0.0, 0.0)
 
-    def peer_col(k):
-        return lax.rem(c + k, n_col)
-
-    def peer_row(k):
-        return lax.rem(r + k, n_row)
+    def peers(n, me, act):
+        half = n // 2
+        act(lax.rem(me + half, n))
+        group = 5 if (half - 1) % 5 == 0 else half - 1
+
+        def some(i, carry):
+            for g in range(group):
+                step = 1 + i * group + g
+                act(lax.rem(me + half + step, n))
+                act(lax.rem(me + half - step, n))
+            return carry
+
+        if half > 1:
+            lax.fori_loop(0, (half - 1) // group, some, 0)
+
+    def col_peers(act):
+        peers(n_col, c, act)
+
+    def row_peers(act):
+        peers(n_row, r, act)
 
     def send(src, dst, phase, lane, device):
         pltpu.make_async_remote_copy(
@@ -401,55 +426,40 @@
 
     barrier = pltpu.get_barrier_semaphore()
 
-    @pl.loop(1, n_col)
-    def _(k):
-        pl.semaphore_signal(barrier, inc=1, device_id={"col": peer_col(k)}, device_id_type=MESH)
-
-    @pl.loop(1, n_row)
-    def _(k):
-        pl.semaphore_signal(barrier, inc=1, device_id={"row": peer_row(k)}, device_id_type=MESH)
+    col_peers(lambda t: pl.semaphore_signal(barrier, inc=1, device_id={"col": t}, device_id_type=MESH))
+    row_peers(lambda t: pl.semaphore_signal(barrier, inc=1, device_id={"row": t}, device_id_type=MESH))
 
     frame = frame_ref[...]
     start = start_ref[...]
+    packed = jnp.concatenate([frame, start], axis=0)
+    pack_buf[...] = packed
+    row_frames[c] = packed
+    col_frames[r] = packed
     mine = rows_of(frame, start)
     ((own1, own2),) = first_product(bufs, entries, [(mine, mine)], [zero3], curves, True)
     own_first = own1 + own2
 
     pl.semaphore_wait(barrier, n_row + n_col - 2)
 
-    def spread(row_src, row_buf, col_src, col_buf, phase):
-        @pl.loop(1, n_col)
-        def _(k):
-            send(row_src, row_buf.at[c], phase, 0, {"col": peer_col(k)})
-
-        @pl.loop(1, n_row)
-        def _(k):
-            send(col_src, col_buf.at[r], phase, 1, {"row": peer_row(k)})
-
-    spread(frame_ref, row_frames, frame_ref, col_frames, 0)
-    spread(start_ref, row_starts, start_ref, col_starts, 1)
-    row_frames[c] = frame
-    col_frames[r] = frame
-    row_starts[c] = start
-    col_starts[r] = start
+    def spread(src, row_buf, col_buf, phase):
+        col_peers(lambda t: send(src, row_buf.at[c], phase, 0, {"col": t}))
+        row_peers(lambda t: send(src, col_buf.at[r], phase, 1, {"row": t}))
+
+    spread(pack_buf, row_frames, col_frames, 0)
     all_wait(row_frames, n_col, recv_sem.at[0, 0])
     all_wait(col_frames, n_row, recv_sem.at[0, 1])
-    all_wait(row_starts, n_col, recv_sem.at[1, 0])
-    all_wait(col_starts, n_row, recv_sem.at[1, 1])
 
     period = (5.0, 5.0, 3.5 * (LANES // 16))
 
     def entry_rows(k, row_vectors, col_vectors):
-        a = list_ref[k, 0]
-        b = list_ref[k, 1]
-        left = rows_of(row_frames[a], row_vectors[a])
-        right = rows_of(col_frames[b], col_vectors[b])
-        return left, right
-
-    tiles = [entry_rows(k, row_starts, col_starts) for k in range(entries)]
-    shifts = [
-        [list_ref[k, 2 + x].astype(jnp.float32) * period[x] for x in range(3)] for k in range(entries)
-    ]
+        a, b = entry[k][0], entry[k][1]
+        left, right = row_frames[a], col_frames[b]
+        if row_vectors is None:
+            return rows_of(left[0:6, :], left[6:12, :]), rows_of(right[0:6, :], right[6:12, :])
+        return rows_of(left[0:6, :], row_vectors[a]), rows_of(right[0:6, :], col_vectors[b])
+
+    tiles = [entry_rows(k, None, None) for k in range(entries)]
+    shifts = [[entry[k][2 + x].astype(jnp.float32) * period[x] for x in range(3)] for k in range(entries)]
     outs = first_product(bufs, 0, tiles, shifts, curves, False)
 
     used = count_ref[0, 0]
@@ -458,35 +468,31 @@
         lefts = [jnp.where(k < used, outs[k][0], 0.0) for k in range(entries)]
         rights = [jnp.where(k < used, outs[k][1], 0.0) for k in range(entries)]
 
-        @pl.loop(0, n_col)
-        def _(t):
-            acc = jnp.zeros((8, LANES), jnp.float32)
-            for k in range(entries):
-                acc = acc + jnp.where(list_ref[k, 0] == t, lefts[k], 0.0)
-            row_out[phase, t] = acc
-
-        @pl.loop(0, n_row)
-        def _(t):
-            acc = jnp.zeros((8, LANES), jnp.float32)
-            for k in range(entries):
-                acc = acc + jnp.where(list_ref[k, 1] == t, rights[k], 0.0)
-            col_out[phase, t] = acc
-
-        @pl.loop(1, n_col)
-        def _(k):
-            t = peer_col(k)
-            send(row_out.at[phase, t], row_buf.at[c], 2 + phase, 0, {"col": t})
-
-        @pl.loop(1, n_row)
-        def _(k):
-            t = peer_row(k)
-            send(col_out.at[phase, t], col_buf.at[r], 2 + phase, 1, {"row": t})
-
-        row_buf[c] = row_out[phase, c]
-        col_buf[r] = col_out[phase, r]
+        def spread_over(n, buf, which, blocks):
+            group = 8 if n % 8 == 0 else n
+
+            def some(i, carry):
+                for g in range(group):
+                    t = i * group + g
+                    acc = None
+                    for k in range(entries):
+                        part = jnp.where(entry[k][which] == t, blocks[k], 0.0)
+                        acc = part if acc is None else acc + part
+                    buf[phase, t] = acc
+                return carry
+
+            lax.fori_loop(0, n // group, some, 0)
+
+        spread_over(n_col, row_out, 0, lefts)
+        spread_over(n_row, col_out, 1, rights)
+        six = pl.ds(0, 6)
+        col_peers(lambda t: send(row_out.at[phase, t, six], row_buf.at[c], 2 + phase, 0, {"col": t}))
+        row_peers(lambda t: send(col_out.at[phase, t, six], col_buf.at[r], 2 + phase, 1, {"row": t}))
+        row_buf[c] = row_out[phase, c, six, :]
+        col_buf[r] = col_out[phase, r, six, :]
         all_wait(row_buf, n_col, recv_sem.at[2 + phase, 0])
         all_wait(col_buf, n_row, recv_sem.at[2 + phase, 1])
-        total = own + jnp.sum(row_buf[...], axis=0) + jnp.sum(col_buf[...], axis=0)
+        total = own[0:6, :] + jnp.sum(row_buf[...], axis=0) + jnp.sum(col_buf[...], axis=0)
         u = [frame[3 + k : 4 + k, :] for k in range(3)]
         twist = cross3(u, [total[3 + k : 4 + k, :] for k in range(3)])
         return jnp.concatenate([total[0:3, :]] + list(twist), axis=0)
@@ -494,17 +500,14 @@
     image = scatter(row_in, col_in, 0, own_first, outs)
 
     image_buf[...] = image
-    spread(image_buf, row_images, image_buf, col_images, 4)
+    spread(image_buf, row_images, col_images, 4)
     row_images[c] = image
     col_images[r] = image
 
     def scalars_out(triple, slot, buf, phase):
         tri_buf[slot] = pack_triple(triple)
 
-        @pl.loop(1, n_row)
-        def _(k):
-            send(tri_buf.at[slot], buf.at[r], phase, 1, {"row": peer_row(k)})
-
+        row_peers(lambda t: send(tri_buf.at[slot], buf.at[r], phase, 1, {"row": t}))
         buf[r] = tri_buf[slot]
 
     def scalars_across(buf, slot, buf2, phase):
@@ -512,10 +515,7 @@
         triple = merge_triples(*unpack_triples(buf[...]), 0)
         tri_buf[slot] = pack_triple(triple)
 
-        @pl.loop(1, n_col)
-        def _(k):
-            send(tri_buf.at[slot], buf2.at[c], phase, 0, {"col": peer_col(k)})
-
+        col_peers(lambda t: send(tri_buf.at[slot], buf2.at[c], phase, 0, {"col": t}))
         buf2[c] = tri_buf[slot]
 
     def scalars_in(buf2, phase):
@@ -561,7 +561,6 @@
 
     for phase, row_buf, col_buf in (
         (0, row_frames, col_frames),
-        (1, row_starts, col_starts),
         (2, row_in, col_in),
         (3, row_in2, col_in2),
         (4, row_images, col_images),
@@ -584,15 +583,15 @@
             return pltpu.VMEM(shape, f32)
 
         scratch = [
+            vm(n_col, 12, LANES), vm(n_row, 12, LANES),
             vm(n_col, 6, LANES), vm(n_row, 6, LANES),
             vm(n_col, 6, LANES), vm(n_row, 6, LANES),
             vm(n_col, 6, LANES), vm(n_row, 6, LANES),
-            vm(n_col, 8, LANES), vm(n_row, 8, LANES),
-            vm(n_col, 8, LANES), vm(n_row, 8, LANES),
             vm(2, n_col, 8, LANES), vm(2, n_row, 8, LANES),
-            vm(n_row, 8, LANES), vm(n_col, 8, LANES),
-            vm(n_row, 8, LANES), vm(n_col, 8, LANES),
-            vm(4, 8, LANES),
+            vm(n_row, 3, LANES), vm(n_col, 3, LANES),
+            vm(n_row, 3, LANES), vm(n_col, 3, LANES),
+            vm(4, 3, LANES),
+            vm(12, LANES),
             vm(6, LANES),
             vm(entries + 1, 8, LANES),
             vm(entries + 1, 12, CHUNK, LANES), vm(entries + 1, 12, CHUNK, LANES),
@@ -620,7 +619,7 @@
             ),
             scratch_shapes=scratch,
             compiler_params=pltpu.CompilerParams(collective_id=0, has_side_effects=True),
-        )(config, start, tile_list.reshape(entries, 5), tile_count)
+        )(config, start, tile_list.transpose(0, 3, 1, 2).reshape(5, 1, entries), tile_count)
 
     placed = (
         P(None, ("row", "col")),

time: 86.3 us -> 75.6 us (0.88)
  Pallas kernels: 81.6 us -> 72.3 us
  local copies, waits for them, and re-layouts: 3.13 us -> 1.78 us
    pallas_call x1, Pallas kernels: 81.6 us -> 72.3 us  [local(): pl.pallas_call(functools.partial(kernel, n_row, n_col), out_shape=(jax.Sh...]
    unnamed x5 -> x4, local copies, waits for them, and re-layouts: 3.13 us -> 1.78 us
where the time goes in v3:
time: 75.6 us; the launch traced here: 75.4 us
  Pallas kernels  72.3 us (96%)
  local copies, waits for them, and re-layouts  1.78 us (2%)
  between operations  1.29 us (2%)
    pallas_call x1, Pallas kernels, local(): pl.pallas_call(functools.partial(kernel, n_row, n_col), out_shape=(jax.Sh...  72.3 us
    unnamed x4, local copies, waits for them, and re-layouts  1.78 us

profile of v3, /device:TPU:1, one launch (start us, length us, event | category | flops | bytes accessed | tf_op | source)
XLA Modules:
  0.0 75.4 jit_solution(8282264892436784868)
XLA Ops:
  1.3 72.3 %shard_map.59 = (f32[4]{0:T(128)}, f32[6,128]{1,0:T(8,128)}) custom-call(f32[6,128]{1,0:T(8,128)} %frame_ref.1, f32[6,128]{1,0:T(8,128)} %start_ref.1, s32[5,1,8]{2,1,0:T(1,128)} %bitcast.3, s32[1,1]{1,0:T(1,128)S(6)} %copy.8.count_ref), custom_call_target="tpu_custom_call" | custom-call | tf_op jit(solution)/shard_map/pallas_call | solution.py:604
  73.6 0.0 copy-start
  73.6 1.2 %copy.9 = f32[4]{0:T(128)} copy(f32[4]{0:T(128)} %get-tuple-element.4) | data formatting | bytes 32
  74.8 0.0 copy-done
  74.8 0.6 copy.10
Async XLA Ops:
  73.6 1.2 %copy-start = (f32[6,128]{1,0:T(8,128)S(1)}, f32[6,128]{1,0:T(8,128)}, u32[]{:S(2)}) copy-start(f32[6,128]{1,0:T(8,128)} %get-tuple-element.5) | copy-start | bytes 9220

commit v4 on v3

--- a/solution.py
+++ b/solution.py
@@ -18,7 +18,7 @@
 CHUNK = 8
 KEPT = 20
 UNROLL_FIRST = 4
-UNROLL_SECOND = 4
+UNROLL_SECOND = 8
 
 
 def dot3(a, b):
@@ -34,33 +34,15 @@
 
 
 def anisotropy(x, spread, tau, A, B, c, norm, twice_cab, prod_tau):
-    t = (2.0 * x) * spread * tau
-    h = 0.5 * t * (norm - x * twice_cab)
+    e = (2.0 * x * x) * spread
+    t = (tau * (1.0 / x)) * e
+    h = t * (0.5 * norm - (0.5 * x) * twice_cab)
     xc = x * c
     gA = t * (xc * B - A)
     gB = t * (xc * A - B)
-    e = (2.0 * x * x) * spread
     gc = e * (prod_tau - c * h)
-    gAB = xc * t
-    gAc = e * (c * gA + B * tau)
-    gBc = e * (c * gB + A * tau)
-    gcc = e * (2.0 * c * gc - h)
-    tau2 = 2.0 * tau
-    gx = tau2 * h
-    first = (gx, gA, gB, gc)
-    second = {
-        (0, 0): -2.0 * tau2 * gx,
-        (0, 1): -tau2 * gA,
-        (0, 2): -tau2 * gB,
-        (0, 3): -tau2 * gc,
-        (1, 1): -t,
-        (1, 2): gAB,
-        (1, 3): gAc,
-        (2, 2): -t,
-        (2, 3): gBc,
-        (3, 3): gcc,
-    }
-    return 1.0 - h, first, second
+    gx = (2.0 * tau) * h
+    return h, (gx, gA, gB, gc), t, e
 
 
 PAIRS = [(p, q) for p in range(4) for q in range(p, 4)]
@@ -78,8 +60,9 @@
     norm = A * A + B * B
     twice_cab = 2.0 * c * AB
     prod_tau = AB * tau
-    g, g1, g2 = anisotropy(chi_shape, D1, tau, A, B, c, norm, twice_cab, prod_tau)
-    q, q1, q2 = anisotropy(chi_energy, D2, tau, A, B, c, norm, twice_cab, prod_tau)
+    hg, g1, tg, eg = anisotropy(chi_shape, D1, tau, A, B, c, norm, twice_cab, prod_tau)
+    hq, q1, tq, eq = anisotropy(chi_energy, D2, tau, A, B, c, norm, twice_cab, prod_tau)
+    g, q = 1.0 - hg, 1.0 - hq
     sigma = lax.rsqrt(g)
     root_g = g * sigma
     alpha = 0.5 * sigma * sigma * sigma
@@ -108,9 +91,29 @@
     tpp = [tp[k] - w1b * G[k] for k in range(4)]
     w1a = w1 * alpha
     w0q = w0 * twice_inv_q
+    tau2 = -2.0 * tau
+    wtq, wtg = w0q * tq, w1a * tg
+    weq, weg = w0q * eq, w1a * eg
+    flat = wtq + wtg
+    upK = up[3] - w0 * lK
+    cw = c * weq, c * weg
+    wet = (weq + weg) * tau
+    cross = wet * B + (cw[0] * q1[1] + cw[1] * g1[1]), wet * A + (cw[0] * q1[2] + cw[1] * g1[2])
+    bent = {
+        (0, 0): (2.0 * tau2) * (w0 * L[0] + w1 * G[0]),
+        (0, 1): tau2 * up[1],
+        (0, 2): tau2 * up[2],
+        (0, 3): tau2 * upK,
+        (1, 1): -flat,
+        (1, 2): c * (chi_energy * wtq + chi_shape * wtg),
+        (1, 3): cross[0],
+        (2, 2): -flat,
+        (2, 3): cross[1],
+        (3, 3): 2.0 * (cw[0] * q1[3] + cw[1] * g1[3]) - (weq * hq + weg * hg),
+    }
     out = []
     for a, b in PAIRS:
-        value = (upp[a] * L[b] + tpp[a] * G[b]) + (w0q * q2[(a, b)] + w1a * g2[(a, b)])
+        value = (upp[a] * L[b] + tpp[a] * G[b]) + bent[(a, b)]
         if b == 3:
             value = value + up[a] * lK
         if (a, b) == (0, 0):
@@ -226,18 +229,14 @@
     trips = slots * groups
     turn_rows(0)
 
-    def first(trip, carry):
-        turn_rows(trip + 1)
-        body(trip)
-        return carry
-
     def later(trip, carry):
         turn_back(trip - 1)
+        body(trip)
         turn_rows(trip + 1)
-        body(trip)
         return carry
 
-    first(0, 0)
+    body(0)
+    turn_rows(1)
     lax.fori_loop(1, trips - 1, later, 0)
     turn_back(trips - 2)
     body(trips - 1)
@@ -374,7 +373,7 @@
 def kernel(
     n_row, n_col,
     frame_ref, start_ref, list_ref, count_ref,
-    coef_ref, mode_ref,
+    out_ref,
     row_frames, col_frames, row_images, col_images,
     row_in, col_in, row_in2, col_in2, row_out, col_out,
     tri_row, tri_col, tri_row2, tri_col2, tri_buf,
@@ -464,7 +463,7 @@
 
     used = count_ref[0, 0]
 
-    def scatter(row_buf, col_buf, phase, own, outs):
+    def scatter(row_buf, col_buf, phase, own, outs, meanwhile):
         lefts = [jnp.where(k < used, outs[k][0], 0.0) for k in range(entries)]
         rights = [jnp.where(k < used, outs[k][1], 0.0) for k in range(entries)]
 
@@ -490,14 +489,15 @@
         row_peers(lambda t: send(col_out.at[phase, t, six], col_buf.at[r], 2 + phase, 1, {"row": t}))
         row_buf[c] = row_out[phase, c, six, :]
         col_buf[r] = col_out[phase, r, six, :]
+        between = meanwhile()
         all_wait(row_buf, n_col, recv_sem.at[2 + phase, 0])
         all_wait(col_buf, n_row, recv_sem.at[2 + phase, 1])
         total = own[0:6, :] + jnp.sum(row_buf[...], axis=0) + jnp.sum(col_buf[...], axis=0)
         u = [frame[3 + k : 4 + k, :] for k in range(3)]
         twist = cross3(u, [total[3 + k : 4 + k, :] for k in range(3)])
-        return jnp.concatenate([total[0:3, :]] + list(twist), axis=0)
-
-    image = scatter(row_in, col_in, 0, own_first, outs)
+        return jnp.concatenate([total[0:3, :]] + list(twist), axis=0), between
+
+    image, _ = scatter(row_in, col_in, 0, own_first, outs, lambda: None)
 
     image_buf[...] = image
     spread(image_buf, row_images, col_images, 4)
@@ -536,16 +536,18 @@
     tiles = [entry_rows(k, row_images, col_images) for k in range(entries)]
     outs = second_product(bufs, 0, tiles, curves)
 
-    image2 = scatter(row_in2, col_in2, 1, own_second, outs)
-
-    F, a, R = scalars_in(tri_col, 5)
-    inv_n0 = lax.rsqrt(F / total_entries + norm_eps)
-    alpha1 = (a * F) * (inv_n0 * inv_n0) / total_entries
-    gap = a - alpha1
-    beta1 = jnp.sqrt((R + gap * gap * F) * (inv_n0 * inv_n0) / total_entries + norm_eps)
-    scale = inv_n0 / beta1
-    second = (image - alpha1 * start) * scale
-    image3 = (image2 - alpha1 * image) * scale - (beta1 * inv_n0) * start
+    def first_scalars():
+        F, a, R = scalars_in(tri_col, 5)
+        inv_n0 = lax.rsqrt(F / total_entries + norm_eps)
+        alpha1 = (a * F) * (inv_n0 * inv_n0) / total_entries
+        gap = a - alpha1
+        beta1 = jnp.sqrt((R + gap * gap * F) * (inv_n0 * inv_n0) / total_entries + norm_eps)
+        scale = inv_n0 / beta1
+        second = (image - alpha1 * start) * scale
+        return alpha1, beta1, second, scale, (alpha1 * scale) * image + (beta1 * inv_n0) * start
+
+    image2, (alpha1, beta1, second, scale, less) = scatter(row_in2, col_in2, 1, own_second, outs, first_scalars)
+    image3 = image2 * scale - less
 
     scalars_out(triple_of(second, image3), 2, tri_row2, 6)
     scalars_across(tri_row2, 3, tri_col2, 6)
@@ -553,11 +555,10 @@
     alpha2 = (a * F) / total_entries
     gap = a - alpha2
     beta2 = jnp.sqrt((R + gap * gap * F) / total_entries + norm_eps)
-    mode_ref[...] = (image3 - alpha2 * second) / beta2
-    coef_ref[0] = alpha1[0, 0]
-    coef_ref[1] = beta1[0, 0]
-    coef_ref[2] = alpha2[0, 0]
-    coef_ref[3] = beta2[0, 0]
+    lane = lax.broadcasted_iota(jnp.int32, (1, LANES), 1)
+    coefs = jnp.where(lane == 0, alpha1, jnp.where(lane == 1, beta1, jnp.where(lane == 2, alpha2, beta2)))
+    out_ref[0:6, :] = (image3 - alpha2 * second) / beta2
+    out_ref[6:8, :] = jnp.broadcast_to(coefs, (2, LANES))
 
     for phase, row_buf, col_buf in (
         (0, row_frames, col_frames),
@@ -569,6 +570,13 @@
     ):
         all_wait(row_buf, n_col, send_sem.at[phase, 0])
         all_wait(col_buf, n_row, send_sem.at[phase, 1])
+
+
+def part_kernel(out_ref, coef_ref, mode_ref):
+    mode_ref[...] = out_ref[0:6, :]
+    row = out_ref[6:7, :]
+    for k in range(4):
+        coef_ref[k] = row[0, k]
 
 
 def solution(mesh):
@@ -601,25 +609,25 @@
             pltpu.SemaphoreType.DMA((7, 2)),
             pltpu.SemaphoreType.DMA((7, 2)),
         ]
-        return pl.pallas_call(
+        out = pl.pallas_call(
             functools.partial(kernel, n_row, n_col),
-            out_shape=(
-                jax.ShapeDtypeStruct((4,), f32),
-                jax.ShapeDtypeStruct((6, LANES), f32),
-            ),
+            out_shape=jax.ShapeDtypeStruct((8, LANES), f32),
             in_specs=[
                 pl.BlockSpec(memory_space=pltpu.VMEM),
                 pl.BlockSpec(memory_space=pltpu.VMEM),
                 pl.BlockSpec(memory_space=pltpu.SMEM),
                 pl.BlockSpec(memory_space=pltpu.SMEM),
             ],
-            out_specs=(
-                pl.BlockSpec(memory_space=pltpu.SMEM),
-                pl.BlockSpec(memory_space=pltpu.VMEM),
-            ),
+            out_specs=pl.BlockSpec(memory_space=pltpu.VMEM),
             scratch_shapes=scratch,
             compiler_params=pltpu.CompilerParams(collective_id=0, has_side_effects=True),
         )(config, start, tile_list.transpose(0, 3, 1, 2).reshape(5, 1, entries), tile_count)
+        return pl.pallas_call(
+            part_kernel,
+            out_shape=(jax.ShapeDtypeStruct((4,), f32), jax.ShapeDtypeStruct((6, LANES), f32)),
+            in_specs=[pl.BlockSpec(memory_space=pltpu.VMEM)],
+            out_specs=(pl.BlockSpec(memory_space=pltpu.SMEM), pl.BlockSpec(memory_space=pltpu.VMEM)),
+        )(out)
 
     placed = (
         P(None, ("row", "col")),

time: 75.6 us -> 69.9 us (0.925)
  Pallas kernels: 72.3 us -> 68.4 us
  local copies, waits for them, and re-layouts: 1.78 us -> 0 us
    pallas_call x1 -> x2, Pallas kernels: 72.3 us -> 68.4 us  [the longest x1 67.1 us: local(): pl.pallas_call(functools.partial(kernel, n_row, n_col), out_shape=jax.Sha...]
    unnamed x4 -> x0, local copies, waits for them, and re-layouts: 1.78 us -> none
where the time goes in v4:
time: 69.9 us; the launch traced here: 69.7 us
  Pallas kernels  68.4 us (98%)
  between operations  1.28 us (2%)
    pallas_call x1, Pallas kernels, local(): pl.pallas_call(functools.partial(kernel, n_row, n_col), out_shape=jax.Sha...  67.1 us

profile of v4, /device:TPU:1, one launch (start us, length us, event | category | flops | bytes accessed | tf_op | source)
XLA Modules:
  0.0 69.7 jit_solution(11076606033524194740)
XLA Ops:
  1.3 67.1 %shard_map.59.out_ref = f32[8,128]{1,0:T(8,128)} custom-call(f32[6,128]{1,0:T(8,128)} %frame_ref.1, f32[6,128]{1,0:T(8,128)} %start_ref.1, s32[5,1,8]{2,1,0:T(1,128)} %bitcast.3, s32[1,1]{1,0:T(1,128)S(6)} %copy.6.count_ref), custom_call_target="tpu_custom_call" | custom-call | tf_op jit(solution)/shard_map/pallas_call | solution.py:612
  68.4 1.3 %shard_map.60 = (f32[4]{0:T(128)}, f32[6,128]{1,0:T(8,128)}) custom-call(f32[8,128]{1,0:T(8,128)} %shard_map.59.out_ref), custom_call_target="tpu_custom_call" | custom-call | tf_op jit(solution)/shard_map/pallas_call | solution.py:625
